TPU v7x, 32 devices: a whole 2x2x4 slice. The times are simulated.
32 devices in a mesh: tm: 16 (over z, x, core), space: 2 (over y).
Axes of the slice: x: 2, y: 2, z: 4, core: 2. Of those that a mesh axis runs over, the one named last changes fastest.
Arguments:
- snapshots: bfloat16 [512, 5, 4096], P('tm', None, 'space'), may hold values from -210 to 210, as said below
- basis: bfloat16 [2, 33, 16, 5, 4096], P(None, None, None, None, ('space', 'tm')), may hold values from -6 to 6
- mass_table: float32 [8, 64, 64], replicated, may hold values from -0.03 to 3, as said below
- elem_kind: int32 [64], P(('space', 'tm')), may hold values from 0 to 7
- offsets: int32 [8], replicated, may hold values from 0 to 256, as said below
Outputs:
- coeffs: float32 [2, 33, 8, 16], replicated
- new_basis: bfloat16 [2, 33, 16, 5, 4096], P(None, None, None, None, ('space', 'tm'))
Inputs may be any that keep to these rules, and one draw needn't show every extreme that they name: `snapshots`: rows of flow data. `mass_table`: each block is symmetric and positive definite. `offsets`: some block starts at 0 and some at 256.
All inputs are finite; a program needn't handle non-finite values.
Results may differ from a plain program's by a relative error of at most 0.0095.
Values may be sent and summed in bfloat16 or wider, within the bound.
A program may use at most 64 MiB of HBM per device.

v0:
```python
import math
import jax
import jax.numpy as jnp
from jax import lax
from jax.sharding import PartitionSpec as P

NT = 256


def spectral_table(offsets, window_len, freq_count, record_len):
    snap_idx = jnp.arange(record_len, dtype=jnp.int32)
    time_lag = snap_idx[None, :] - offsets[:, None]
    inside = (time_lag >= 0) & (time_lag < window_len)
    lag_clip = jnp.clip(time_lag, 0, window_len - 1)
    lag_float = lag_clip.astype(jnp.float32)
    hann_wt = 0.5 - 0.5 * jnp.cos(2.0 * math.pi / window_len * lag_float)
    norm_wt = 1.0 / math.sqrt(0.375 * window_len)
    freq_idx = jnp.arange(freq_count, dtype=jnp.int32)
    phase_int = jnp.mod(freq_idx[:, None, None] * lag_clip[None], window_len)
    angle = 2.0 * math.pi / window_len * phase_int.astype(jnp.float32)
    weight = jnp.where(inside, hann_wt * norm_wt, jnp.zeros_like(hann_wt))[None]
    real_part = weight * jnp.cos(angle)
    imag_part = -weight * jnp.sin(angle)
    return jnp.stack([real_part, imag_part]).astype(jnp.bfloat16)


def apply_mass(field, local_mass):
    lead = field.shape[:-1]
    elem_count = local_mass.shape[0]
    shaped = field.reshape(lead + (elem_count, local_mass.shape[1]))
    result = jnp.einsum("...ep,epq->...eq", shaped, local_mass, precision=lax.Precision.HIGHEST)
    return result.reshape(field.shape)


def paired_einsum(pattern, first_pair, second_pair):
    real_out = jnp.einsum(
        pattern, first_pair[0], second_pair[0], preferred_element_type=jnp.float32
    ) + jnp.einsum(pattern, first_pair[1], second_pair[1], preferred_element_type=jnp.float32)
    imag_out = jnp.einsum(
        pattern, first_pair[0], second_pair[1], preferred_element_type=jnp.float32
    ) - jnp.einsum(pattern, first_pair[1], second_pair[0], preferred_element_type=jnp.float32)
    return (real_out, imag_out)


def on_device(snapshots, basis, mass_table, elem_kind, offsets):
    regrouped = lax.all_to_all(snapshots, "tm", split_axis=2, concat_axis=0, tiled=True)
    record_len, var_count, local_pts = regrouped.shape
    freq_count = basis.shape[1]
    mode_count = basis.shape[2]
    block_total = offsets.shape[0]
    kind_count = mass_table.shape[0]
    flat_len = var_count * local_pts
    entries = flat_len * lax.axis_size("tm") * lax.axis_size("space")
    dft_table = spectral_table(offsets, NT, freq_count, record_len)
    record_flat = regrouped.reshape(record_len, flat_len)
    spectra = jnp.dot(
        dft_table.reshape(2 * freq_count * block_total, record_len),
        record_flat,
        preferred_element_type=jnp.float32,
    )
    selector = (elem_kind[:, None] == jnp.arange(kind_count, dtype=jnp.int32)[None, :]).astype(
        jnp.float32
    )
    local_mass = jnp.einsum("ek,kpq->epq", selector, mass_table, precision=lax.Precision.HIGHEST)
    spectra = spectra.reshape(2, freq_count, block_total, var_count, local_pts)
    weighted = (
        apply_mass(spectra, local_mass)
        .astype(jnp.bfloat16)
        .reshape(2, freq_count, block_total, flat_len)
    )
    mode_rows = basis.reshape(2, freq_count, mode_count, flat_len)
    coeff_real, coeff_imag = paired_einsum("fkx,fbx->fbk", mode_rows, weighted)
    coeff_part = jnp.stack([coeff_real, coeff_imag])
    spec_round = spectra.astype(jnp.bfloat16).reshape(2, freq_count, block_total, flat_len)
    gram_real, gram_imag = paired_einsum("fbx,fcx->fbc", spec_round, weighted)
    coeff_sum, gram_real, gram_imag = lax.psum((coeff_part, gram_real, gram_imag), ("tm", "space"))
    coeffs = coeff_sum / math.sqrt(entries)
    table_float = dft_table.astype(jnp.float32)
    coeff_round = lax.optimization_barrier(coeffs.astype(jnp.bfloat16)).astype(jnp.float32)
    kernel_real = jnp.einsum("fbt,fbk->fkt", table_float[0], coeff_round[0]) - jnp.einsum(
        "fbt,fbk->fkt", table_float[1], coeff_round[1]
    )
    kernel_imag = jnp.einsum("fbt,fbk->fkt", table_float[0], coeff_round[1]) + jnp.einsum(
        "fbt,fbk->fkt", table_float[1], coeff_round[0]
    )
    kernel = (
        jnp.stack([kernel_real, kernel_imag])
        .astype(jnp.bfloat16)
        .reshape(2 * freq_count * mode_count, record_len)
    )
    fields = jnp.dot(kernel, record_flat, preferred_element_type=jnp.float32)
    fields = fields.reshape(2, freq_count, mode_count, var_count, local_pts)
    apply_real = jnp.einsum("fbc,fck->fbk", gram_real, coeff_round[0]) - jnp.einsum(
        "fbc,fck->fbk", gram_imag, coeff_round[1]
    )
    apply_imag = jnp.einsum("fbc,fck->fbk", gram_real, coeff_round[1]) + jnp.einsum(
        "fbc,fck->fbk", gram_imag, coeff_round[0]
    )
    energy = jnp.sum(coeff_round[0] * apply_real + coeff_round[1] * apply_imag, axis=1)
    factor = 1.0 / jnp.sqrt(energy / entries + 1e-06)
    new_basis = (fields * factor[None, :, :, None, None]).astype(jnp.bfloat16)
    return (coeffs, new_basis)


def solution(mesh):
    return jax.shard_map(
        on_device,
        mesh=mesh,
        in_specs=(
            P("tm", None, "space"),
            P(None, None, None, None, ("space", "tm")),
            P(),
            P(("space", "tm")),
            P(),
        ),
        out_specs=(P(), P(None, None, None, None, ("space", "tm"))),
        check_vma=False,
    )
```

profile of v0, /device:TPU:0, one launch (start us, length us, event | category | flops | bytes accessed | tf_op | source)
XLA Modules:
  0.0 120.1 jit_solution(16826947783138899716)
XLA Ops:
  0.6 5.4 %copy.35 = bf16[32,5,2048]{0,1,2:T(8,128)(2,1)} copy(bf16[32,5,2048]{2,0,1:T(8,128)(2,1)} %param.5) | data formatting | bytes 1310720 | tf_op args[0]
  6.0 5.2 %reshape.176 = bf16[16,2,10240]{2,1,0:T(2,128)(2,1)} reshape(bf16[2048,5,32]{2,1,0:T(8,128)(2,1)} %bitcast.99) | data formatting | bytes 1310720
  11.3 7.4 %all-to-all-start = ((bf16[16,2,10240]{2,1,0:T(2,128)(2,1)}), bf16[16,2,10240]{2,1,0:T(2,128)(2,1)S(1)}, u32[]{:S(2)}, u32[]{:S(2)}) async-start(bf16[16,2,10240]{2,1,0:T(2,128)(2,1)} %reshape.176), calls=%async_computation | async-start | bytes 1310720 | tf_op jit(solution)/shard_map/all_to_all | solution.py:46
  19.2 1.6 %squeeze.25 = bf16[33,16,640]{2,1,0:T(8,128)(2,1)} reshape(bf16[1,33,16,5,128]{4,3,2,1,0:T(8,128)(2,1)S(1)} %copy.40) | data formatting | bytes 1351680 | tf_op jit(solution)/shard_map/squeeze | solution.py:37
  21.1 1.7 %squeeze.27 = bf16[33,16,640]{2,1,0:T(8,128)(2,1)} reshape(bf16[1,33,16,5,128]{4,3,2,1,0:T(8,128)(2,1)S(1)} %copy.42) | data formatting | bytes 1351680 | tf_op jit(solution)/shard_map/squeeze | solution.py:38
  22.8 0.4 convolution_bitcast_fusion
  23.4 2.2 %multiply_convert_fusion.2 = (bf16[1,33,8,512]{3,2,1,0:T(8,128)(2,1)S(1)}, bf16[1,33,8,512]{3,2,1,0:T(8,128)(2,1)S(1)}) fusion(s32[8,512]{1,0:T(8,128)S(1)} %fusion.42, f32[8,512]{1,0:T(8,128)S(1)} %get-tuple-element.21, f32[8,512]{1,0:T(8,128)S(1)} %get-tuple-element.22), kind=kLoop, calls=%fused_computation.38 | loop fusion | flops 2433024 | bytes 589824 | tf_op jit(solution)/shard_map/slice | solution.py:80
  25.7 9.5 %all-to-all-done = bf16[16,2,10240]{2,1,0:T(2,128)(2,1)S(1)} async-done(((bf16[16,2,10240]{2,1,0:T(2,128)(2,1)}), bf16[16,2,10240]{2,1,0:T(2,128)(2,1)S(1)}, u32[]{:S(2)}, u32[]{:S(2)}) %all-to-all-start) | async-done | bytes 655392 | tf_op jit(solution)/shard_map/all_to_all | solution.py:46
  35.2 4.0 %reshape.177 = bf16[2048,5,32]{2,1,0:T(8,128)(2,1)} reshape(bf16[16,2,10240]{2,1,0:T(2,128)(2,1)S(1)} %all-to-all-done) | data formatting | bytes 1310720
  39.2 4.5 %copy.36 = bf16[32,5,16,128]{3,1,0,2:T(8,128)(2,1)S(1)} copy(bf16[32,5,16,128]{0,1,3,2:T(8,128)(2,1)} %bitcast.98) | data formatting | bytes 1310720 | tf_op jit(solution)/shard_map/all_to_all | solution.py:46
  43.7 1.9 %fusion.70 = (bf16[528,640]{1,0:T(8,128)(2,1)}, f32[528,640]{1,0:T(8,128)}) fusion(bf16[528,512]{1,0:T(8,128)(2,1)S(1)} %bitcast.103, bf16[64,8,5,128]{3,2,1,0:T(8,128)(2,1)S(1)} %bitcast.100), kind=kOutput, calls=%fused_computation.95 | convolution fusion | flops 346368000 | bytes 3223552 | tf_op jit(solution)/shard_map/dot_general | solution.py:56
  45.6 3.1 %reshape_reshape.3 = f32[2,33,8,5,2,64]{5,4,3,2,1,0:T(2,128)S(1)} reshape(f32[528,640]{1,0:T(8,128)} %get-tuple-element.24) | data formatting | bytes 2703360 | tf_op jit(solution)/shard_map/reshape;reshape | solution.py:30
  48.7 3.5 %fusion.5 = bf16[2,33,8,5,2,64]{5,1,3,2,0,4:T(8,128)(2,1)S(1)} fusion(f32[2,33,8,5,2,64]{5,4,3,2,1,0:T(2,128)S(1)} %reshape_reshape.3, f32[2,64,64,1,1,1]{2,0,1,5,4,3:T(2,128)S(1)} %convolution_bitcast_fusion), kind=kOutput, calls=%fused_computation.4 | convolution fusion | flops 259860480 | bytes 2060288 | tf_op jit(solution)/shard_map/...ep,epq->...eq/dot_general | solution.py:31
  52.5 0.7 copy.41
  53.2 0.4 squeeze.26
  53.6 0.7 copy.39
  54.3 0.4 squeeze.24
  57.7 48.1 %all-reduce = (f32[2,33,8,16]{3,2,1,0:T(8,128)S(1)}, bf16[33,8,8]{2,1,0:T(8,128)(2,1)S(1)}, bf16[33,8,8]{2,1,0:T(8,128)(2,1)S(1)}) all-reduce(f32[2,33,8,16]{3,2,1,0:T(8,128)S(1)} %pad_maximum_fusion.1, f32[33,8,8]{2,1,0:T(8,128)S(1)} %convolution_add_fusion.1, ...), channel_id=1, replica_groups=mesh['tm'=16,'space'=2] {'tm','space'}, use_global_device_ids=true, to_apply=%region_0.1 | all-reduce | flops 12672 | bytes 92928 | tf_op jit(solution)/shard_map/psum | solution.py:76
  105.9 2.0 %fusion.33 = f32[33,16,512]{2,1,0:T(8,128)S(1)} fusion(s32[8,512]{1,0:T(8,128)S(1)} %fusion.42, f32[8,512]{1,0:T(8,128)S(1)} %get-tuple-element.21, bf16[2,33,8,16]{3,2,1,0:T(8,128)(2,1)S(1)} %get-tuple-element.17), kind=kOutput, calls=%fused_computation.50 | convolution fusion | flops 6488064 | bytes 1181696 | tf_op jit(solution)/shard_map/fbt,fbk->fkt/dot_general | solution.py:80
  107.9 2.0 %fusion.31 = f32[33,16,512]{2,1,0:T(8,128)S(1)} fusion(s32[8,512]{1,0:T(8,128)S(1)} %fusion.42, f32[8,512]{1,0:T(8,128)S(1)} %get-tuple-element.21, bf16[2,33,8,16]{3,2,1,0:T(8,128)(2,1)S(1)} %get-tuple-element.17), kind=kOutput, calls=%fused_computation.48 | convolution fusion | flops 6488064 | bytes 1181696 | tf_op jit(solution)/shard_map/fbt,fbk->fkt/dot_general | solution.py:83
  110.5 3.0 %fusion.11 = bf16[1,33,16,512]{3,2,1,0:T(8,128)(2,1)} fusion(f32[33,16,512]{2,1,0:T(8,128)S(1)} %fusion.33, f32[8,512]{1,0:T(8,128)S(1)} %get-tuple-element.22, s32[8,512]{1,0:T(8,128)S(1)} %fusion.42, bf16[2,33,8,16]{3,2,1,0:T(8,128)(2,1)S(1)} %get-tuple-element.17), kind=kOutput, calls=%fused_computation.10 | convolution fusion | flops 7028736 | bytes 1722368 | tf_op jit(solution)/shard_map/fbt,fbk->fkt/dot_general | solution.py:80
  113.5 3.0 %fusion.10 = bf16[1,33,16,512]{3,2,1,0:T(8,128)(2,1)} fusion(f32[33,16,512]{2,1,0:T(8,128)S(1)} %fusion.31, f32[8,512]{1,0:T(8,128)S(1)} %get-tuple-element.22, s32[8,512]{1,0:T(8,128)S(1)} %fusion.42, bf16[2,33,8,16]{3,2,1,0:T(8,128)(2,1)S(1)} %get-tuple-element.17), kind=kOutput, calls=%fused_computation.9 | convolution fusion | flops 7028736 | bytes 1722368 | tf_op jit(solution)/shard_map/fbt,fbk->fkt/dot_general | solution.py:83
  117.1 0.8 copy.44
  118.0 2.1 %multiply_convert_fusion = bf16[2,33,16,5,128]{4,2,3,1,0:T(8,128)(2,1)} fusion(bf16[5,128,512,1,1]{2,1,0,4,3:T(8,128)(2,1)S(1)} %bitcast.104, f32[33,16]{1,0:T(8,128)S(1)} %add_rsqrt_fusion, bf16[1,33,16,512]{3,2,1,0:T(8,128)(2,1)S(1)} %copy-done.10, bf16[1,33,16,512]{3,2,1,0:T(8,128)(2,1)S(1)} %copy-done.9), kind=kOutput, calls=%fused_computation.2 | convolution fusion | flops 695574528 | bytes 3090496 | tf_op jit(solution)/shard_map/dot_general | solution.py:91
  (47 shorter events, 5.4 us)
Async XLA Ops:
  0.6 22.2 %copy-start = (f32[8,64,64]{2,1,0:T(8,128)S(1)}, f32[8,64,64]{2,1,0:T(8,128)}, u32[]{:S(2)}) copy-start(f32[8,64,64]{2,1,0:T(8,128)} %param.7) | copy-start | bytes 393220
  6.0 12.6 %copy-start.6 = (bf16[2,33,16,5,128]{4,2,3,1,0:T(8,128)(2,1)S(1)}, bf16[2,33,16,5,128]{4,2,3,1,0:T(8,128)(2,1)}, u32[]{:S(2)}) copy-start(bf16[2,33,16,5,128]{4,2,3,1,0:T(8,128)(2,1)} %param.6) | copy-start | bytes 4055044
  11.3 24.0 %all-to-all-start = ((bf16[16,2,10240]{2,1,0:T(2,128)(2,1)}), bf16[16,2,10240]{2,1,0:T(2,128)(2,1)S(1)}, u32[]{:S(2)}, u32[]{:S(2)}) async-start(bf16[16,2,10240]{2,1,0:T(2,128)(2,1)} %reshape.176), calls=%async_computation | async-start | bytes 1310720 | tf_op jit(solution)/shard_map/all_to_all | solution.py:46
  20.8 2.0 %copy-start.8 = (s32[2]{0:T(128)S(1)}, s32[2]{0:T(128)}, u32[]{:S(2)}) copy-start(s32[2]{0:T(128)} %param.8) | copy-start | bytes 28
  21.1 2.1 %copy-start.7 = (s32[8]{0:T(128)S(1)}, s32[8]{0:T(128)}, u32[]{:S(2)}) copy-start(s32[8]{0:T(128)} %param.9) | copy-start | bytes 100
  43.6 1.9 %copy-start.1 = (bf16[32,5,16,128]{3,1,0,2:T(8,128)(2,1)}, bf16[32,5,16,128]{3,1,0,2:T(8,128)(2,1)S(1)}, u32[]{:S(2)}) copy-start(bf16[32,5,16,128]{3,1,0,2:T(8,128)(2,1)S(1)} %copy.36) | copy-start | bytes 1966084
  53.6 1.1 copy-start.5
  54.3 1.1 copy-start.4
  55.9 1.1 copy-start.3
  107.9 2.4 %copy-start.2 = (bf16[32,5,16,128]{3,1,0,2:T(8,128)(2,1)S(1)}, bf16[32,5,16,128]{3,1,0,2:T(8,128)(2,1)}, u32[]{:S(2)}) copy-start(bf16[32,5,16,128]{3,1,0,2:T(8,128)(2,1)} %copy-done.1) | copy-start | bytes 1966084
  116.5 1.5 %copy-start.9 = (bf16[1,33,16,512]{3,2,1,0:T(8,128)(2,1)S(1)}, bf16[1,33,16,512]{3,2,1,0:T(8,128)(2,1)}, u32[]{:S(2)}) copy-start(bf16[1,33,16,512]{3,2,1,0:T(8,128)(2,1)} %fusion.11) | copy-start | bytes 1622020
  116.5 1.5 %copy-start.10 = (bf16[1,33,16,512]{3,2,1,0:T(8,128)(2,1)S(1)}, bf16[1,33,16,512]{3,2,1,0:T(8,128)(2,1)}, u32[]{:S(2)}) copy-start(bf16[1,33,16,512]{3,2,1,0:T(8,128)(2,1)} %fusion.10) | copy-start | bytes 1622020
where the time goes:
time: 121 us; the launch traced here: 120 us
  blocking collectives  48.1 us (40%)
  local copies, waits for them, and re-layouts  30.1 us (25%)
  matrix products  21.4 us (18%)
  waiting for transfers between devices  9.49 us (8%)
  starting transfers between devices  7.39 us (6%)
  other arithmetic  2.59 us (2%)
    psum x1, blocking collectives, on_device(): lax.psum((coeff_part, gram_real, gram_imag), ('tm', 'space'))  48.1 us
    unnamed x27, local copies, waits for them, and re-layouts  15.7 us
    all_to_all x1, waiting for transfers between devices, on_device(): lax.all_to_all(snapshots, 'tm', split_axis=2, concat_axis=0, tiled=True)  9.49 us
    all_to_all x1, starting transfers between devices, on_device(): lax.all_to_all(snapshots, 'tm', split_axis=2, concat_axis=0, tiled=True)  7.39 us
    all_to_all x1, local copies, waits for them, and re-layouts, on_device(): lax.all_to_all(snapshots, 'tm', split_axis=2, concat_axis=0, tiled=True)  4.46 us
    dot_general x1, matrix products, apply_mass(): jnp.einsum('...ep,epq->...eq', shaped, local_mass, precision=lax.Precisio...  3.49 us
    another operation x1, local copies, waits for them, and re-layouts, apply_mass(): shaped = field.reshape(lead + (elem_count, local_mass.shape[1]))  3.11 us
    dot_general x1, matrix products, on_device(): jnp.einsum('fbt,fbk->fkt', table_float[1], coeff_round[1])  3.02 us
  transfers between devices with their start and end apart: 1, of which 1 were waited for; matrix products, arithmetic and copies ran while one was open for 6% of the time, Pallas kernels for 0%

commit v1 on v0

--- a/solution.py
+++ b/solution.py
@@ -73,7 +73,9 @@
     coeff_part = jnp.stack([coeff_real, coeff_imag])
     spec_round = spectra.astype(jnp.bfloat16).reshape(2, freq_count, block_total, flat_len)
     gram_real, gram_imag = paired_einsum("fbx,fcx->fbc", spec_round, weighted)
-    coeff_sum, gram_real, gram_imag = lax.psum((coeff_part, gram_real, gram_imag), ("tm", "space"))
+    coeff_sum, gram_real, gram_imag = lax.psum(
+        lax.psum((coeff_part, gram_real, gram_imag), "space"), "tm"
+    )
     coeffs = coeff_sum / math.sqrt(entries)
     table_float = dft_table.astype(jnp.float32)
     coeff_round = lax.optimization_barrier(coeffs.astype(jnp.bfloat16)).astype(jnp.float32)

time: 121 us -> 156 us (1.29)
  blocking collectives: 48.1 us -> 84.1 us
    psum x1 -> x2, blocking collectives: 48.1 us -> 84.1 us  [the longest x1 66.3 us: on_device(): lax.psum(lax.psum((coeff_part, gram_real, gram_imag), 'space'), 'tm')]
    unnamed x27 -> x25, local copies, waits for them, and re-layouts: 15.7 us -> 15.8 us
  transfers between devices with their start and end apart: 1 -> 1, of which waited for: 1 -> 1; matrix products, arithmetic and copies ran while one was open for 6% -> 5% of each run, Pallas kernels for 0% -> 0%
where the time goes in v1:
time: 156 us; the launch traced here: 155 us
  blocking collectives  84.1 us (54%)
  local copies, waits for them, and re-layouts  30.2 us (19%)
  matrix products  20.7 us (13%)
  waiting for transfers between devices  9.49 us (6%)
  starting transfers between devices  7.39 us (5%)
  other arithmetic  2.59 us (2%)
    psum x1, blocking collectives, on_device(): lax.psum(lax.psum((coeff_part, gram_real, gram_imag), 'space'), 'tm')  66.3 us
    psum x1, blocking collectives, on_device(): lax.psum((coeff_part, gram_real, gram_imag), 'space')  17.8 us
    unnamed x25, local copies, waits for them, and re-layouts  15.8 us
    all_to_all x1, waiting for transfers between devices, on_device(): lax.all_to_all(snapshots, 'tm', split_axis=2, concat_axis=0, tiled=True)  9.49 us
    all_to_all x1, starting transfers between devices, on_device(): lax.all_to_all(snapshots, 'tm', split_axis=2, concat_axis=0, tiled=True)  7.39 us
    all_to_all x1, local copies, waits for them, and re-layouts, on_device(): lax.all_to_all(snapshots, 'tm', split_axis=2, concat_axis=0, tiled=True)  4.46 us
    dot_general x1, matrix products, apply_mass(): jnp.einsum('...ep,epq->...eq', shaped, local_mass, precision=lax.Precisio...  3.49 us
  transfers between devices with their start and end apart: 1, of which 1 were waited for; matrix products, arithmetic and copies ran while one was open for 5% of the time, Pallas kernels for 0%

profile of v1, /device:TPU:0, one launch (start us, length us, event | category | flops | bytes accessed | tf_op | source)
XLA Modules:
  0.0 155.4 jit_solution(7317628550784300448)
XLA Ops:
  0.6 5.4 %copy.35 = bf16[32,5,2048]{0,1,2:T(8,128)(2,1)} copy(bf16[32,5,2048]{2,0,1:T(8,128)(2,1)} %param.5) | data formatting | bytes 1310720 | tf_op args[0]
  6.0 5.2 %reshape.176 = bf16[16,2,10240]{2,1,0:T(2,128)(2,1)} reshape(bf16[2048,5,32]{2,1,0:T(8,128)(2,1)} %bitcast.99) | data formatting | bytes 1310720
  11.3 7.4 %all-to-all-start = ((bf16[16,2,10240]{2,1,0:T(2,128)(2,1)}), bf16[16,2,10240]{2,1,0:T(2,128)(2,1)S(1)}, u32[]{:S(2)}, u32[]{:S(2)}) async-start(bf16[16,2,10240]{2,1,0:T(2,128)(2,1)} %reshape.176), calls=%async_computation | async-start | bytes 1310720 | tf_op jit(solution)/shard_map/all_to_all | solution.py:46
  19.2 1.6 %squeeze.25 = bf16[33,16,640]{2,1,0:T(8,128)(2,1)} reshape(bf16[1,33,16,5,128]{4,3,2,1,0:T(8,128)(2,1)S(1)} %copy.40) | data formatting | bytes 1351680 | tf_op jit(solution)/shard_map/squeeze | solution.py:37
  21.1 1.7 %squeeze.27 = bf16[33,16,640]{2,1,0:T(8,128)(2,1)} reshape(bf16[1,33,16,5,128]{4,3,2,1,0:T(8,128)(2,1)S(1)} %copy.42) | data formatting | bytes 1351680 | tf_op jit(solution)/shard_map/squeeze | solution.py:38
  22.8 0.4 convolution_bitcast_fusion
  23.5 2.2 %multiply_convert_fusion.2 = (bf16[1,33,8,512]{3,2,1,0:T(8,128)(2,1)S(1)}, bf16[1,33,8,512]{3,2,1,0:T(8,128)(2,1)S(1)}) fusion(s32[8,512]{1,0:T(8,128)S(1)} %fusion.42, f32[8,512]{1,0:T(8,128)S(1)} %get-tuple-element.24, f32[8,512]{1,0:T(8,128)S(1)} %get-tuple-element.25), kind=kLoop, calls=%fused_computation.38 | loop fusion | flops 2433024 | bytes 589824 | tf_op jit(solution)/shard_map/slice | solution.py:82
  25.7 9.5 %all-to-all-done = bf16[16,2,10240]{2,1,0:T(2,128)(2,1)S(1)} async-done(((bf16[16,2,10240]{2,1,0:T(2,128)(2,1)}), bf16[16,2,10240]{2,1,0:T(2,128)(2,1)S(1)}, u32[]{:S(2)}, u32[]{:S(2)}) %all-to-all-start) | async-done | bytes 655392 | tf_op jit(solution)/shard_map/all_to_all | solution.py:46
  35.2 4.0 %reshape.177 = bf16[2048,5,32]{2,1,0:T(8,128)(2,1)} reshape(bf16[16,2,10240]{2,1,0:T(2,128)(2,1)S(1)} %all-to-all-done) | data formatting | bytes 1310720
  39.2 4.5 %copy.36 = bf16[32,5,16,128]{3,1,0,2:T(8,128)(2,1)S(1)} copy(bf16[32,5,16,128]{0,1,3,2:T(8,128)(2,1)} %bitcast.98) | data formatting | bytes 1310720 | tf_op jit(solution)/shard_map/all_to_all | solution.py:46
  43.7 1.9 %fusion.70 = (bf16[528,640]{1,0:T(8,128)(2,1)}, f32[528,640]{1,0:T(8,128)}) fusion(bf16[528,512]{1,0:T(8,128)(2,1)S(1)} %bitcast.103, bf16[64,8,5,128]{3,2,1,0:T(8,128)(2,1)S(1)} %bitcast.100), kind=kOutput, calls=%fused_computation.95 | convolution fusion | flops 346368000 | bytes 3223552 | tf_op jit(solution)/shard_map/dot_general | solution.py:56
  45.6 3.1 %reshape_reshape.3 = f32[2,33,8,5,2,64]{5,4,3,2,1,0:T(2,128)S(1)} reshape(f32[528,640]{1,0:T(8,128)} %get-tuple-element.27) | data formatting | bytes 2703360 | tf_op jit(solution)/shard_map/reshape;reshape | solution.py:30
  48.7 3.5 %fusion.5 = bf16[2,33,8,5,2,64]{5,1,3,2,0,4:T(8,128)(2,1)S(1)} fusion(f32[2,33,8,5,2,64]{5,4,3,2,1,0:T(2,128)S(1)} %reshape_reshape.3, f32[2,64,64,1,1,1]{2,0,1,5,4,3:T(2,128)S(1)} %convolution_bitcast_fusion), kind=kOutput, calls=%fused_computation.4 | convolution fusion | flops 259860480 | bytes 2060288 | tf_op jit(solution)/shard_map/...ep,epq->...eq/dot_general | solution.py:31
  52.5 0.7 copy.41
  53.2 0.4 squeeze.26
  53.6 0.7 copy.39
  57.7 17.8 %all-reduce.1 = (f32[2,33,8,16]{3,2,1,0:T(8,128)S(1)}, f32[33,8,8]{2,1,0:T(8,128)S(1)}, f32[33,8,8]{2,1,0:T(8,128)S(1)}) all-reduce(f32[2,33,8,16]{3,2,1,0:T(8,128)S(1)} %pad_maximum_fusion.1, f32[33,8,8]{2,1,0:T(8,128)S(1)} %convolution_add_fusion.1, ...), channel_id=1, replica_groups=mesh['tm'=16,'space'=2] {'space'}, use_global_device_ids=true, to_apply=%region_0.1 | all-reduce | flops 12672 | bytes 101376 | tf_op jit(solution)/shard_map/psum | solution.py:77
  75.5 66.3 %all-reduce = (f32[2,33,8,16]{3,2,1,0:T(8,128)S(1)}, bf16[33,8,8]{2,1,0:T(8,128)(2,1)S(1)}, bf16[33,8,8]{2,1,0:T(8,128)(2,1)S(1)}) all-reduce(f32[2,33,8,16]{3,2,1,0:T(8,128)S(1)} %get-tuple-element.13, f32[33,8,8]{2,1,0:T(8,128)S(1)} %get-tuple-element.14, ...), channel_id=1, replica_groups=mesh['tm'=16,'space'=2] {'tm'}, use_global_device_ids=true, to_apply=%region_1.2 | all-reduce | flops 12672 | bytes 92928 | tf_op jit(solution)/shard_map/psum | solution.py:76
  141.9 2.0 %fusion.33 = f32[33,16,512]{2,1,0:T(8,128)S(1)} fusion(s32[8,512]{1,0:T(8,128)S(1)} %fusion.42, f32[8,512]{1,0:T(8,128)S(1)} %get-tuple-element.24, bf16[2,33,8,16]{3,2,1,0:T(8,128)(2,1)S(1)} %get-tuple-element.20), kind=kOutput, calls=%fused_computation.50 | convolution fusion | flops 6488064 | bytes 1181696 | tf_op jit(solution)/shard_map/fbt,fbk->fkt/dot_general | solution.py:82
  143.9 2.0 %fusion.31 = f32[33,16,512]{2,1,0:T(8,128)S(1)} fusion(s32[8,512]{1,0:T(8,128)S(1)} %fusion.42, f32[8,512]{1,0:T(8,128)S(1)} %get-tuple-element.24, bf16[2,33,8,16]{3,2,1,0:T(8,128)(2,1)S(1)} %get-tuple-element.20), kind=kOutput, calls=%fused_computation.48 | convolution fusion | flops 6488064 | bytes 1181696 | tf_op jit(solution)/shard_map/fbt,fbk->fkt/dot_general | solution.py:85
  146.5 2.3 %fusion.11 = bf16[1,33,16,512]{3,2,1,0:T(8,128)(2,1)S(1)} fusion(f32[33,16,512]{2,1,0:T(8,128)S(1)} %fusion.33, f32[8,512]{1,0:T(8,128)S(1)} %get-tuple-element.25, s32[8,512]{1,0:T(8,128)S(1)} %fusion.42, bf16[2,33,8,16]{3,2,1,0:T(8,128)(2,1)S(1)} %get-tuple-element.20), kind=kOutput, calls=%fused_computation.10 | convolution fusion | flops 7028736 | bytes 1722368 | tf_op jit(solution)/shard_map/fbt,fbk->fkt/dot_general | solution.py:82
  148.8 3.0 %fusion.10 = bf16[1,33,16,512]{3,2,1,0:T(8,128)(2,1)} fusion(f32[33,16,512]{2,1,0:T(8,128)S(1)} %fusion.31, f32[8,512]{1,0:T(8,128)S(1)} %get-tuple-element.25, s32[8,512]{1,0:T(8,128)S(1)} %fusion.42, bf16[2,33,8,16]{3,2,1,0:T(8,128)(2,1)S(1)} %get-tuple-element.20), kind=kOutput, calls=%fused_computation.9 | convolution fusion | flops 7028736 | bytes 1722368 | tf_op jit(solution)/shard_map/fbt,fbk->fkt/dot_general | solution.py:85
  152.4 0.8 copy.44
  153.3 2.1 %multiply_convert_fusion = bf16[2,33,16,5,128]{4,2,3,1,0:T(8,128)(2,1)} fusion(bf16[5,128,512,1,1]{2,1,0,4,3:T(8,128)(2,1)S(1)} %bitcast.104, f32[33,16]{1,0:T(8,128)S(1)} %add_rsqrt_fusion, bf16[1,33,16,512]{3,2,1,0:T(8,128)(2,1)S(1)} %copy-done.9, bf16[1,33,16,512]{3,2,1,0:T(8,128)(2,1)S(1)} %fusion.11), kind=kOutput, calls=%fused_computation.2 | convolution fusion | flops 695574528 | bytes 3090496 | tf_op jit(solution)/shard_map/dot_general | solution.py:93
  (46 shorter events, 5.8 us)
Async XLA Ops:
  0.6 22.2 %copy-start = (f32[8,64,64]{2,1,0:T(8,128)S(1)}, f32[8,64,64]{2,1,0:T(8,128)}, u32[]{:S(2)}) copy-start(f32[8,64,64]{2,1,0:T(8,128)} %param.7) | copy-start | bytes 393220
  6.0 12.6 %copy-start.6 = (bf16[2,33,16,5,128]{4,2,3,1,0:T(8,128)(2,1)S(1)}, bf16[2,33,16,5,128]{4,2,3,1,0:T(8,128)(2,1)}, u32[]{:S(2)}) copy-start(bf16[2,33,16,5,128]{4,2,3,1,0:T(8,128)(2,1)} %param.6) | copy-start | bytes 4055044
  11.3 24.0 %all-to-all-start = ((bf16[16,2,10240]{2,1,0:T(2,128)(2,1)}), bf16[16,2,10240]{2,1,0:T(2,128)(2,1)S(1)}, u32[]{:S(2)}, u32[]{:S(2)}) async-start(bf16[16,2,10240]{2,1,0:T(2,128)(2,1)} %reshape.176), calls=%async_computation | async-start | bytes 1310720 | tf_op jit(solution)/shard_map/all_to_all | solution.py:46
  20.8 2.0 %copy-start.8 = (s32[2]{0:T(128)S(1)}, s32[2]{0:T(128)}, u32[]{:S(2)}) copy-start(s32[2]{0:T(128)} %param.8) | copy-start | bytes 28
  21.1 2.1 %copy-start.7 = (s32[8]{0:T(128)S(1)}, s32[8]{0:T(128)}, u32[]{:S(2)}) copy-start(s32[8]{0:T(128)} %param.9) | copy-start | bytes 100
  43.7 1.9 %copy-start.1 = (bf16[32,5,16,128]{3,1,0,2:T(8,128)(2,1)}, bf16[32,5,16,128]{3,1,0,2:T(8,128)(2,1)S(1)}, u32[]{:S(2)}) copy-start(bf16[32,5,16,128]{3,1,0,2:T(8,128)(2,1)S(1)} %copy.36) | copy-start | bytes 1966084
  53.6 1.1 copy-start.5
  54.4 1.1 copy-start.4
  55.9 1.1 copy-start.3
  143.9 2.4 %copy-start.2 = (bf16[32,5,16,128]{3,1,0,2:T(8,128)(2,1)S(1)}, bf16[32,5,16,128]{3,1,0,2:T(8,128)(2,1)}, u32[]{:S(2)}) copy-start(bf16[32,5,16,128]{3,1,0,2:T(8,128)(2,1)} %copy-done.1) | copy-start | bytes 1966084
  151.8 1.5 copy-start.9
